TPU v7x, 128 devices: a whole 4x4x4 slice. The times are simulated.
128 devices in a mesh: side: 2 (over core), grp: 8 (over x_hi, y), tp: 8 (over x_lo, z).
Axes of the slice: x: 4 (x_hi: 2, x_lo: 2; x = x_hi * 2 + x_lo), y: 4, z: 4, core: 2. Of those that a mesh axis runs over, the one named last changes fastest.
Arguments:
- queries: bfloat16 [192, 4096], P('grp', 'side'), may hold values from -6 to 6
- kv_cache: bfloat16 [192, 16, 192, 256], P('grp', ('side', 'tp')), may hold values from -6 to 6
- lengths: int32 [192], P('grp'), may hold values from 2 to 768, as said below
- out_weight: bfloat16 [4096, 2048], P(('side', 'tp')), may hold values from -1 to 1
- resid: bfloat16 [192, 2048], P('grp'), may hold values from -6 to 6
- norm_gain: float32 [2048], replicated, may hold values from 0.1 to 1.9
- expert_ids: int32 [192, 8], P('grp'), may hold values from 0 to 127, all different within a row; in each aligned block of 24 rows (0 to 23, 24 to 47, ...) at most 3 rows name the same one
- expert_gates: float32 [192, 8], P('grp'), may hold values from 0.05 to 1
- w_gate_up: bfloat16 [128, 2048, 1536], P(('side', 'grp', 'tp')), may hold values from -0.125 to 0.125
- w_down: bfloat16 [128, 768, 2048], P(('side', 'grp', 'tp')), may hold values from -0.21875 to 0.21875
Outputs:
- layer_out: bfloat16 [192, 2048], P('grp', ('side', 'tp'))
Inputs may be any that keep to these rules, and one draw needn't show every extreme that they name: `lengths`: every row's cache holds at least two tokens; some row holds exactly 768. `expert_ids`: each row names 8 different experts. Among the rows of one row group no expert is named by more than 3 rows; in some group an expert is named by exactly 3.
All inputs are finite; a program needn't handle non-finite values.
Results may differ from a plain program's by a relative error of at most 0.017.
Values may be sent and summed in bfloat16 or wider, within the bound.
A program may use at most 64 MiB of HBM per device.

v0:
```python
import math
import jax
import jax.numpy as jnp
from jax import lax
from jax.sharding import PartitionSpec as P

QH = 32
KVH = 4
HD = 128
TOPK = 8


def swapped(value, axis, distance):
    mask = 2**distance
    pairs = [(source, source ^ mask) for source in range(lax.axis_size(axis))]
    return lax.ppermute(value, axis, pairs)


def body(
    queries,
    kv_cache,
    lengths,
    out_weight,
    resid,
    norm_gain,
    expert_ids,
    expert_gates,
    w_gate_up,
    w_down,
):
    lane_count = lax.axis_size("tp")
    tp_index = lax.axis_index("tp")
    side_count = lax.axis_size("side")
    section = lax.axis_index("side")
    grp_count = lax.axis_size("grp")
    group_size = side_count * lane_count
    member_index = section * lane_count + tp_index
    kv_parts = group_size // KVH
    group_heads = QH // KVH
    per_member = QH // group_size
    part_span = kv_cache.shape[2]
    model_width = out_weight.shape[1]
    piece_width = model_width // group_size
    rows_grp = lengths.shape[0]
    local_experts = w_gate_up.shape[0]
    experts_all = local_experts * side_count * grp_count * lane_count
    capacity = max(2, 2 * rows_grp * TOPK // experts_all)
    head_start = tp_index // kv_parts * group_heads * HD
    part_index = tp_index % kv_parts
    row_count = queries.shape[0]
    query_rows = lax.dynamic_slice_in_dim(queries, head_start, group_heads * HD, 1).reshape(
        row_count, group_heads, HD
    )
    key_rows = kv_cache[:, 0, :, :HD]
    value_rows = kv_cache[:, 0, :, HD:]
    positions = part_index * part_span + jnp.arange(part_span, dtype=jnp.int32)
    valid_mask = (positions[None, :] < lengths[:, None])[:, None, :]
    scores = jnp.einsum(
        "rgd,rpd->rgp", query_rows, key_rows, preferred_element_type=jnp.float32
    ) / math.sqrt(HD)
    scores = jnp.where(valid_mask, scores, -1e30)
    row_max = jnp.max(scores, axis=-1)
    for bit_index in range(kv_parts.bit_length() - 1):
        row_max = jnp.maximum(row_max, swapped(row_max, "tp", bit_index))
    weights = jnp.where(valid_mask, jnp.exp(scores - row_max[..., None]), 0.0)
    weight_sum = jnp.sum(weights, axis=-1)
    numerator = jnp.einsum(
        "rgp,rpd->rgd", weights.astype(jnp.bfloat16), value_rows, preferred_element_type=jnp.float32
    )
    for bit_index in range(kv_parts.bit_length() - 1):
        other_numerator, other_sum = swapped((numerator, weight_sum), "tp", bit_index)
        numerator = numerator + other_numerator
        weight_sum = weight_sum + other_sum
    heads_out = (numerator / weight_sum[..., None]).astype(jnp.bfloat16)
    mine = lax.dynamic_slice_in_dim(heads_out, part_index * per_member, per_member, 1).reshape(
        row_count, per_member * HD
    )
    projected = jnp.dot(mine, out_weight, preferred_element_type=jnp.float32)
    summed = lax.psum(projected, ("side", "tp"))
    middle = (resid.astype(jnp.float32) + summed).astype(jnp.bfloat16)
    middle_wide = middle.astype(jnp.float32)
    inv_rms = lax.rsqrt(jnp.mean(middle_wide * middle_wide, axis=-1, keepdims=True) + 1e-06)
    normed = (middle_wide * inv_rms * norm_gain).astype(jnp.bfloat16)
    column_experts = (
        (
            (section * grp_count + jnp.arange(grp_count, dtype=jnp.int32)[:, None]) * lane_count
            + tp_index
        )
        * local_experts
        + jnp.arange(local_experts, dtype=jnp.int32)[None, :]
    ).reshape(-1)
    matches = expert_ids[:, :, None] == column_experts[None, None, :]
    hit_count = jnp.sum(matches.astype(jnp.int32), axis=1)
    gate_cols = jnp.sum(jnp.where(matches, expert_gates[:, :, None], 0.0), axis=1)
    slot_rank = jnp.cumsum(hit_count, axis=0) - hit_count
    slot_ids = jnp.arange(capacity, dtype=jnp.int32)
    placed = (hit_count[:, :, None] == 1) & (slot_rank[:, :, None] == slot_ids[None, None, :])
    send_map = placed.astype(jnp.bfloat16)
    outgoing = jnp.einsum(
        "rcs,rd->csd", send_map, normed, preferred_element_type=jnp.float32
    ).astype(jnp.bfloat16)
    outgoing = outgoing.reshape(grp_count, local_experts, capacity, model_width)
    hidden = jnp.einsum(
        "gjcd,jdf->gjcf",
        lax.all_to_all(outgoing, "grp", split_axis=0, concat_axis=0, tiled=True),
        w_gate_up,
        preferred_element_type=jnp.float32,
    )
    inner_width = hidden.shape[-1] // 2
    activated = (jax.nn.silu(hidden[..., :inner_width]) * hidden[..., inner_width:]).astype(
        jnp.bfloat16
    )
    produced = jnp.einsum(
        "gjcf,jfd->gjcd", activated, w_down, preferred_element_type=jnp.float32
    ).astype(jnp.bfloat16)
    returned = lax.all_to_all(produced, "grp", split_axis=0, concat_axis=0, tiled=True)
    combine_weights = (send_map.astype(jnp.float32) * gate_cols[:, :, None]).reshape(row_count, -1)
    moe_part = jnp.dot(
        combine_weights,
        returned.reshape(-1, model_width).astype(jnp.float32),
        precision=lax.Precision.HIGHEST,
    )
    middle_mine = lax.dynamic_slice_in_dim(middle_wide, member_index * piece_width, piece_width, 1)
    moe_whole = lax.psum(moe_part, ("side", "tp"))
    return (
        middle_mine
        + lax.dynamic_slice_in_dim(moe_whole, member_index * piece_width, piece_width, 1)
    ).astype(jnp.bfloat16)


def solution(mesh):
    in_specs = (
        P("grp", "side"),
        P("grp", ("side", "tp"), None, None),
        P("grp"),
        P(("side", "tp"), None),
        P("grp", None),
        P(),
        P("grp", None),
        P("grp", None),
        P(("side", "grp", "tp"), None, None),
        P(("side", "grp", "tp"), None, None),
    )
    out_specs = P("grp", ("side", "tp"))
    return jax.shard_map(body, mesh=mesh, in_specs=in_specs, out_specs=out_specs, check_vma=False)
```

profile of v0, /device:TPU:1, one launch (start us, length us, event | category | flops | bytes accessed | tf_op | source)
XLA Modules:
  0.0 333.3 jit_solution(7118665528007655057)
XLA Ops:
  6.5 0.0 copy-start
  6.5 0.0 all-reduce.3.cloned.1.call-start
  6.6 1.0 dynamic-slice_bitcast_fusion
  7.5 0.7 broadcast_compare_fusion
  8.3 2.1 fusion.47
  10.3 2.5 collective-permute-start
  12.8 0.8 fusion.34
  13.6 0.3 collective-permute-done
  13.9 3.4 %collective-permute-start.1 = (f32[24,8]{1,0:T(8,128)S(1)}, f32[24,8]{1,0:T(8,128)S(1)}, u32[]{:S(2)}, u32[]{:S(2)}) collective-permute-start(f32[24,8]{1,0:T(8,128)S(1)} %max.6), channel_id=1, source_target_pairs={{0,2},{1,3},{2,0},{3,1},{4,6},{5,7},{6,4},{7,5},{8,10},{9,11},{10,... | collective-permute-start | bytes 2312 | tf_op jit(solution)/shard_map/ppermute | solution.py:16
  17.3 0.6 broadcast_compare_fusion.1
  17.9 0.6 collective-permute-done.1
  18.5 0.2 fusion.18
  18.7 1.0 collective-permute-start.4
  19.7 1.7 fusion.14
  21.4 0.5 collective-permute-start.2
  22.0 0.0 collective-permute-done.4
  22.0 2.9 collective-permute-start.5
  24.9 0.0 copy-done.3
  24.9 0.8 fusion.35
  25.7 0.1 copy.37
  25.8 0.1 copy.39
  25.9 1.1 collective-permute-done.5
  27.0 0.0 collective-permute-done.2
  27.0 2.0 collective-permute-start.3
  29.1 0.1 constant_dynamic-slice_fusion
  29.1 2.9 collective-permute-done.3
  32.1 0.1 fusion.37
  32.2 2.2 fusion.39
  34.4 0.0 all-reduce.3.cloned.1.call-update
  34.4 1.3 convert_multiply_fusion
  35.7 130.8 %all-reduce.3.cloned.1.call-done = f32[24,2048]{1,0:T(8,128)} async-done(((f32[24,2048]{1,0:T(8,128)}), f32[24,2048]{1,0:T(8,128)}) %all-reduce.3.cloned.1.call-update) | async-done | bytes 196624 | tf_op jit(solution)/shard_map/psum | solution.py:79
  166.5 0.0 copy-done.1
  166.5 1.1 multiply_reduce_fusion
  167.5 0.9 fusion.10
  168.5 0.1 copy.41
  168.6 13.4 %all_to_all.10 = bf16[8,1,3,2048]{3,2,1,0:T(4,128)(2,1)S(1)} all-to-all(bf16[8,1,3,2048]{3,2,1,0:T(4,128)(2,1)S(1)} %copy.41), channel_id=1, replica_groups=mesh['side'=2,'grp'=8,'tp'=8] {'grp'}, dimensions={0} | all-to-all | bytes 196608 | tf_op jit(solution)/shard_map/all_to_all | solution.py:105
  182.0 3.7 %fusion.4 = f32[8,1,3,1536]{3,0,2,1:T(8,128)S(1)} fusion(bf16[1,2048,1536]{2,1,0:T(8,128)(2,1)} %param.18, bf16[8,1,3,2048]{3,2,1,0:T(4,128)(2,1)S(1)} %all_to_all.10), kind=kOutput, calls=%fused_computation.4 | convolution fusion | flops 150994944 | bytes 6537216 | tf_op jit(solution)/shard_map/gjcd,jdf->gjcf/dot_general | solution.py:103
  185.7 0.0 copy-start.2
  185.7 0.5 fusion.11
  186.2 0.7 copy.43
  187.0 3.4 %all-to-all-start.1 = ((bf16[8,1,3,2048]{3,2,1,0:T(4,128)(2,1)}), bf16[8,1,3,2048]{3,2,1,0:T(4,128)(2,1)S(1)}, u32[]{:S(2)}, u32[]{:S(2)}) async-start(bf16[8,1,3,2048]{3,2,1,0:T(4,128)(2,1)} %copy.43), calls=%async_computation.1 | async-start | bytes 262144 | tf_op jit(solution)/shard_map/all_to_all | solution.py:116
  190.3 0.0 all-reduce.5.cloned.1.call-start
  190.4 6.8 %all-to-all-done.1 = bf16[8,1,3,2048]{3,2,1,0:T(4,128)(2,1)S(1)} async-done(((bf16[8,1,3,2048]{3,2,1,0:T(4,128)(2,1)}), bf16[8,1,3,2048]{3,2,1,0:T(4,128)(2,1)S(1)}, u32[]{:S(2)}, u32[]{:S(2)}) %all-to-all-start.1) | async-done | bytes 98336 | tf_op jit(solution)/shard_map/all_to_all | solution.py:116
  197.2 0.7 reshape.139
  197.9 1.9 fusion.48
  199.8 0.0 all-reduce.5.cloned.1.call-update
  199.8 125.3 %all-reduce.5.cloned.1.call-done = f32[24,2048]{1,0:T(8,128)} async-done(((f32[24,2048]{1,0:T(8,128)}), f32[24,2048]{1,0:T(8,128)}) %all-reduce.5.cloned.1.call-update) | async-done | bytes 196624 | tf_op jit(solution)/shard_map/psum | solution.py:124
  325.1 1.3 add_convert_fusion.1
  (16 shorter events, 0.1 us)
Async XLA Ops:
  6.5 179.2 %copy-start = (bf16[1,768,2048]{2,1,0:T(8,128)(2,1)S(1)}, bf16[1,768,2048]{2,1,0:T(8,128)(2,1)}, u32[]{:S(2)}) copy-start(bf16[1,768,2048]{2,1,0:T(8,128)(2,1)} %param.19) | copy-start | bytes 9437188
  6.5 18.4 %copy-start.3 = (s32[24,8]{0,1:T(8,128)S(1)}, s32[24,8]{0,1:T(8,128)}, u32[]{:S(2)}) copy-start(s32[24,8]{0,1:T(8,128)} %param.16) | copy-start | bytes 2308
  6.5 159.9 %all-reduce.3.cloned.1.call-start = ((), (), s32[]{:S(2)}) async-start(), calls=%async_computation.2 | async-start | bytes 393216 | tf_op jit(solution)/shard_map/psum | solution.py:79
  8.3 158.2 %copy-start.1 = (bf16[24,2048]{1,0:T(8,128)(2,1)S(1)}, bf16[24,2048]{1,0:T(8,128)(2,1)}, u32[]{:S(2)}) copy-start(bf16[24,2048]{1,0:T(8,128)(2,1)} %param.14) | copy-start | bytes 294916
  10.3 3.6 %collective-permute-start = (f32[24,8]{1,0:T(8,128)S(1)}, f32[24,8]{1,0:T(8,128)S(1)}, u32[]{:S(2)}, u32[]{:S(2)}) collective-permute-start(f32[24,8]{1,0:T(8,128)S(1)} %get-tuple-element.9), channel_id=1, source_target_pairs={{0,1},{1,0},{2,3},{3,2},{4,5},{5,4},{6,7},{7,6},{8,9},{9,8},{10,11... | collective-permute-start | bytes 2312 | tf_op jit(solution)/shard_map/ppermute | solution.py:16
  13.9 4.6 %collective-permute-start.1 = (f32[24,8]{1,0:T(8,128)S(1)}, f32[24,8]{1,0:T(8,128)S(1)}, u32[]{:S(2)}, u32[]{:S(2)}) collective-permute-start(f32[24,8]{1,0:T(8,128)S(1)} %max.6), channel_id=1, source_target_pairs={{0,2},{1,3},{2,0},{3,1},{4,6},{5,7},{6,4},{7,5},{8,10},{9,11},{10,... | collective-permute-start | bytes 2312 | tf_op jit(solution)/shard_map/ppermute | solution.py:16
  18.7 3.3 collective-permute-start.4
  21.4 5.6 %collective-permute-start.2 = (f32[24,8,128]{2,1,0:T(8,128)S(1)}, f32[24,8,128]{2,1,0:T(8,128)S(1)}, u32[]{:S(2)}, u32[]{:S(2)}) collective-permute-start(f32[24,8,128]{2,1,0:T(8,128)S(1)} %fusion.14), channel_id=1, source_target_pairs={{0,1},{1,0},{2,3},{3,2},{4,5},{5,4},{6,7},{7,6},{8,9},{9,8},{10,11... | collective-permute-start | bytes 294920 | tf_op jit(solution)/shard_map/ppermute | solution.py:16
  22.0 5.0 %collective-permute-start.5 = (f32[24,8]{1,0:T(8,128)S(1)}, f32[24,8]{1,0:T(8,128)S(1)}, u32[]{:S(2)}, u32[]{:S(2)}) collective-permute-start(f32[24,8]{1,0:T(8,128)S(1)} %add.92), channel_id=1, source_target_pairs={{0,2},{1,3},{2,0},{3,1},{4,6},{5,7},{6,4},{7,5},{8,10},{9,11},{10,... | collective-permute-start | bytes 2312 | tf_op jit(solution)/shard_map/ppermute | solution.py:16
  27.0 5.1 %collective-permute-start.3 = (f32[24,8,128]{2,1,0:T(8,128)S(1)}, f32[24,8,128]{2,1,0:T(8,128)S(1)}, u32[]{:S(2)}, u32[]{:S(2)}) collective-permute-start(f32[24,8,128]{2,1,0:T(8,128)S(1)} %add.90), channel_id=1, source_target_pairs={{0,2},{1,3},{2,0},{3,1},{4,6},{5,7},{6,4},{7,5},{8,10},{9,11},{10,... | collective-permute-start | bytes 294920 | tf_op jit(solution)/shard_map/ppermute | solution.py:16
  185.7 4.7 %copy-start.2 = (f32[24,8,3]{0,2,1:T(4,128)S(1)}, f32[24,8,3]{0,2,1:T(4,128)}, u32[]{:S(2)}) copy-start(f32[24,8,3]{0,2,1:T(4,128)} %get-tuple-element.7) | copy-start | bytes 6916
  187.0 10.3 %all-to-all-start.1 = ((bf16[8,1,3,2048]{3,2,1,0:T(4,128)(2,1)}), bf16[8,1,3,2048]{3,2,1,0:T(4,128)(2,1)S(1)}, u32[]{:S(2)}, u32[]{:S(2)}) async-start(bf16[8,1,3,2048]{3,2,1,0:T(4,128)(2,1)} %copy.43), calls=%async_computation.1 | async-start | bytes 262144 | tf_op jit(solution)/shard_map/all_to_all | solution.py:116
  190.3 134.8 %all-reduce.5.cloned.1.call-start = ((), (), s32[]{:S(2)}) async-start(), calls=%async_computation.3 | async-start | bytes 393216 | tf_op jit(solution)/shard_map/psum | solution.py:124
Sparse Core Ops, SparseCore 0:
  34.5 131.9 all-reduce.2
  199.9 125.1 all-reduce.4
where the time goes:
time: 334 us; the launch traced here: 333 us
  waiting for transfers between devices  268 us (80%)
  starting transfers between devices  15.9 us (5%)
  between operations  13.5 us (4%)
  blocking collectives  13.4 us (4%)
  matrix products  13 us (4%)
  other arithmetic  6.89 us (2%)
    psum x1, waiting for transfers between devices, body(): summed = lax.psum(projected, ('side', 'tp'))  131 us
    psum x1, waiting for transfers between devices, body(): moe_whole = lax.psum(moe_part, ('side', 'tp'))  125 us
    all_to_all x1, blocking collectives, body(): lax.all_to_all(outgoing, 'grp', split_axis=0, concat_axis=0, tiled=True)  13.4 us
    ppermute x6, starting transfers between devices, swapped(): return lax.ppermute(value, axis, pairs)  12.4 us
    all_to_all x1, waiting for transfers between devices, body(): lax.all_to_all(produced, 'grp', split_axis=0, concat_axis=0, tiled=True)  6.8 us
  transfers between devices with their start and end apart: 9, of which 7 were waited for; matrix products, arithmetic and copies ran while one was open for 2% of the time, Pallas kernels for 0%

commit v1 on v0

--- a/solution.py
+++ b/solution.py
@@ -76,7 +76,7 @@
         row_count, per_member * HD
     )
     projected = jnp.dot(mine, out_weight, preferred_element_type=jnp.float32)
-    summed = lax.psum(projected, ("side", "tp"))
+    summed = jnp.sum(lax.all_gather(projected, ("side", "tp")), axis=0)
     middle = (resid.astype(jnp.float32) + summed).astype(jnp.bfloat16)
     middle_wide = middle.astype(jnp.float32)
     inv_rms = lax.rsqrt(jnp.mean(middle_wide * middle_wide, axis=-1, keepdims=True) + 1e-06)

time: 334 us -> 248 us (0.74)
  waiting for transfers between devices: 268 us -> 182 us
    psum x1 -> x0, waiting for transfers between devices: 131 us -> none  [body(): summed = lax.psum(projected, ('side', 'tp'))]
    all_gather x0 -> x1, waiting for transfers between devices: none -> 43.3 us  [body(): summed = jnp.sum(lax.all_gather(projected, ('side', 'tp')), axis=0)]
  transfers between devices with their start and end apart: 9 -> 9, of which waited for: 7 -> 8; matrix products, arithmetic and copies ran while one was open for 2% -> 1% of each run, Pallas kernels for 0% -> 0%
where the time goes in v1:
time: 248 us
  waiting for transfers between devices  182 us (73%)
  starting transfers between devices  17.2 us (7%)
  between operations  13.5 us (5%)
  matrix products  13 us (5%)
  blocking collectives  12.9 us (5%)
  other arithmetic  6.28 us (3%)
  local copies, waits for them, and re-layouts  2.75 us (1%)
    psum x1, waiting for transfers between devices, body(): moe_whole = lax.psum(moe_part, ('side', 'tp'))  125 us
    all_gather x1, waiting for transfers between devices, body(): summed = jnp.sum(lax.all_gather(projected, ('side', 'tp')), axis=0)  43.3 us
    ppermute x6, starting transfers between devices, swapped(): return lax.ppermute(value, axis, pairs)  13.8 us
    all_to_all x1, blocking collectives, body(): lax.all_to_all(outgoing, 'grp', split_axis=0, concat_axis=0, tiled=True)  12.9 us
    ppermute x6, waiting for transfers between devices, swapped(): return lax.ppermute(value, axis, pairs)  7.4 us
    all_to_all x1, waiting for transfers between devices, body(): lax.all_to_all(produced, 'grp', split_axis=0, concat_axis=0, tiled=True)  6.81 us
  transfers between devices with their start and end apart: 9, of which 8 were waited for; matrix products, arithmetic and copies ran while one was open for 1% of the time, Pallas kernels for 0%

profile of v1, /device:TPU:1, one launch (start us, length us, event | category | flops | bytes accessed | tf_op | source)
XLA Modules:
  0.0 247.7 jit_solution(8369777246671961106)
XLA Ops:
  6.5 0.0 copy-start
  6.5 0.0 all-gather.3.cloned.1.call-start
  6.6 1.0 dynamic-slice_bitcast_fusion
  7.6 0.7 broadcast_compare_fusion
  8.3 2.1 fusion.47
  10.4 2.5 %collective-permute-start = (f32[24,8]{1,0:T(8,128)S(1)}, f32[24,8]{1,0:T(8,128)S(1)}, u32[]{:S(2)}, u32[]{:S(2)}) collective-permute-start(f32[24,8]{1,0:T(8,128)S(1)} %get-tuple-element.9), channel_id=1, source_target_pairs={{0,1},{1,0},{2,3},{3,2},{4,5},{5,4},{6,7},{7,6},{8,9},{9,8},{10,11... | collective-permute-start | bytes 2312 | tf_op jit(solution)/shard_map/ppermute | solution.py:16
  12.8 1.1 collective-permute-done
  13.9 3.4 %collective-permute-start.1 = (f32[24,8]{1,0:T(8,128)S(1)}, f32[24,8]{1,0:T(8,128)S(1)}, u32[]{:S(2)}, u32[]{:S(2)}) collective-permute-start(f32[24,8]{1,0:T(8,128)S(1)} %max.6), channel_id=1, source_target_pairs={{0,2},{1,3},{2,0},{3,1},{4,6},{5,7},{6,4},{7,5},{8,10},{9,11},{10,... | collective-permute-start | bytes 2312 | tf_op jit(solution)/shard_map/ppermute | solution.py:16
  17.3 1.1 collective-permute-done.1
  18.5 1.7 fusion.14
  20.2 1.0 collective-permute-start.2
  21.2 0.2 fusion.18
  21.4 0.6 collective-permute-start.4
  22.0 2.0 collective-permute-done.4
  24.0 3.3 %collective-permute-start.5 = (f32[24,8]{1,0:T(8,128)S(1)}, f32[24,8]{1,0:T(8,128)S(1)}, u32[]{:S(2)}, u32[]{:S(2)}) collective-permute-start(f32[24,8]{1,0:T(8,128)S(1)} %add.90), channel_id=1, source_target_pairs={{0,2},{1,3},{2,0},{3,1},{4,6},{5,7},{6,4},{7,5},{8,10},{9,11},{10,... | collective-permute-start | bytes 2312 | tf_op jit(solution)/shard_map/ppermute | solution.py:16
  27.3 1.1 collective-permute-done.5
  28.4 0.0 collective-permute-done.2
  28.4 3.0 %collective-permute-start.3 = (f32[24,8,128]{2,1,0:T(8,128)S(1)}, f32[24,8,128]{2,1,0:T(8,128)S(1)}, u32[]{:S(2)}, u32[]{:S(2)}) collective-permute-start(f32[24,8,128]{2,1,0:T(8,128)S(1)} %add.88), channel_id=1, source_target_pairs={{0,2},{1,3},{2,0},{3,1},{4,6},{5,7},{6,4},{7,5},{8,10},{9,11},{10,... | collective-permute-start | bytes 294920 | tf_op jit(solution)/shard_map/ppermute | solution.py:16
  31.5 0.1 constant_dynamic-slice_fusion
  31.5 2.1 collective-permute-done.3
  33.6 0.1 fusion.37
  33.7 2.2 fusion.39
  35.9 0.0 all-gather.3.cloned.1.call-update
  35.9 0.0 copy-done.1
  35.9 0.1 fusion.34
  36.0 0.1 copy.37
  36.1 0.1 copy.39
  36.2 0.0 copy-done.2
  36.2 0.1 fusion.35
  36.3 0.6 convert_multiply_fusion
  36.9 43.3 %all-gather.3.cloned.1.call-done = f32[384,2048]{1,0:T(8,128)} async-done(((f32[24,2048]{1,0:T(8,128)}), f32[384,2048]{1,0:T(8,128)}) %all-gather.3.cloned.1.call-update) | async-done | bytes 3145744 | tf_op jit(solution)/shard_map/all_gather | solution.py:79
  80.2 2.1 reduce_sum.46
  82.2 1.0 multiply_reduce_fusion
  83.3 0.9 fusion.10
  84.2 0.1 copy.41
  84.3 12.9 %all_to_all.10 = bf16[8,1,3,2048]{3,2,1,0:T(4,128)(2,1)S(1)} all-to-all(bf16[8,1,3,2048]{3,2,1,0:T(4,128)(2,1)S(1)} %copy.41), channel_id=1, replica_groups=mesh['side'=2,'grp'=8,'tp'=8] {'grp'}, dimensions={0} | all-to-all | bytes 196608 | tf_op jit(solution)/shard_map/all_to_all | solution.py:105
  97.2 3.7 %fusion.4 = f32[8,1,3,1536]{3,0,2,1:T(8,128)S(1)} fusion(bf16[1,2048,1536]{2,1,0:T(8,128)(2,1)} %param.18, bf16[8,1,3,2048]{3,2,1,0:T(4,128)(2,1)S(1)} %all_to_all.10), kind=kOutput, calls=%fused_computation.4 | convolution fusion | flops 150994944 | bytes 6537216 | tf_op jit(solution)/shard_map/gjcd,jdf->gjcf/dot_general | solution.py:103
  100.9 0.0 copy-done
  100.9 0.5 fusion.11
  101.5 0.7 copy.43
  102.2 3.4 %all-to-all-start.1 = ((bf16[8,1,3,2048]{3,2,1,0:T(4,128)(2,1)}), bf16[8,1,3,2048]{3,2,1,0:T(4,128)(2,1)S(1)}, u32[]{:S(2)}, u32[]{:S(2)}) async-start(bf16[8,1,3,2048]{3,2,1,0:T(4,128)(2,1)} %copy.43), calls=%async_computation.1 | async-start | bytes 262144 | tf_op jit(solution)/shard_map/all_to_all | solution.py:116
  105.6 0.0 all-reduce.2.cloned.1.call-start
  105.6 6.8 %all-to-all-done.1 = bf16[8,1,3,2048]{3,2,1,0:T(4,128)(2,1)S(1)} async-done(((bf16[8,1,3,2048]{3,2,1,0:T(4,128)(2,1)}), bf16[8,1,3,2048]{3,2,1,0:T(4,128)(2,1)S(1)}, u32[]{:S(2)}, u32[]{:S(2)}) %all-to-all-start.1) | async-done | bytes 98336 | tf_op jit(solution)/shard_map/all_to_all | solution.py:116
  112.5 0.7 reshape.139
  113.2 1.8 fusion.48
  115.0 0.0 all-reduce.2.cloned.1.call-update
  115.0 124.5 %all-reduce.2.cloned.1.call-done = f32[24,2048]{1,0:T(8,128)} async-done(((f32[24,2048]{1,0:T(8,128)}), f32[24,2048]{1,0:T(8,128)}) %all-reduce.2.cloned.1.call-update) | async-done | bytes 196624 | tf_op jit(solution)/shard_map/psum | solution.py:124
  239.6 1.3 add_convert_fusion.1
  (15 shorter events, 0.1 us)
Async XLA Ops:
  6.5 94.4 %copy-start = (bf16[1,768,2048]{2,1,0:T(8,128)(2,1)S(1)}, bf16[1,768,2048]{2,1,0:T(8,128)(2,1)}, u32[]{:S(2)}) copy-start(bf16[1,768,2048]{2,1,0:T(8,128)(2,1)} %param.19) | copy-start | bytes 9437188
  6.5 29.4 %copy-start.1 = (s32[24,8]{0,1:T(8,128)S(1)}, s32[24,8]{0,1:T(8,128)}, u32[]{:S(2)}) copy-start(s32[24,8]{0,1:T(8,128)} %param.16) | copy-start | bytes 2308
  6.5 29.7 %copy-start.2 = (f32[24,8]{0,1:T(8,128)S(1)}, f32[24,8]{0,1:T(8,128)}, u32[]{:S(2)}) copy-start(f32[24,8]{0,1:T(8,128)} %param.17) | copy-start | bytes 2308
  6.5 73.6 %all-gather.3.cloned.1.call-start = ((), (), s32[]{:S(2)}) async-start(), calls=%async_computation.3 | async-start | bytes 3342336 | tf_op jit(solution)/shard_map/all_gather | solution.py:79
  10.4 3.6 %collective-permute-start = (f32[24,8]{1,0:T(8,128)S(1)}, f32[24,8]{1,0:T(8,128)S(1)}, u32[]{:S(2)}, u32[]{:S(2)}) collective-permute-start(f32[24,8]{1,0:T(8,128)S(1)} %get-tuple-element.9), channel_id=1, source_target_pairs={{0,1},{1,0},{2,3},{3,2},{4,5},{5,4},{6,7},{7,6},{8,9},{9,8},{10,11... | collective-permute-start | bytes 2312 | tf_op jit(solution)/shard_map/ppermute | solution.py:16
  13.9 4.6 %collective-permute-start.1 = (f32[24,8]{1,0:T(8,128)S(1)}, f32[24,8]{1,0:T(8,128)S(1)}, u32[]{:S(2)}, u32[]{:S(2)}) collective-permute-start(f32[24,8]{1,0:T(8,128)S(1)} %max.6), channel_id=1, source_target_pairs={{0,2},{1,3},{2,0},{3,1},{4,6},{5,7},{6,4},{7,5},{8,10},{9,11},{10,... | collective-permute-start | bytes 2312 | tf_op jit(solution)/shard_map/ppermute | solution.py:16
  20.2 8.2 %collective-permute-start.2 = (f32[24,8,128]{2,1,0:T(8,128)S(1)}, f32[24,8,128]{2,1,0:T(8,128)S(1)}, u32[]{:S(2)}, u32[]{:S(2)}) collective-permute-start(f32[24,8,128]{2,1,0:T(8,128)S(1)} %fusion.14), channel_id=1, source_target_pairs={{0,1},{1,0},{2,3},{3,2},{4,5},{5,4},{6,7},{7,6},{8,9},{9,8},{10,11... | collective-permute-start | bytes 294920 | tf_op jit(solution)/shard_map/ppermute | solution.py:16
  21.4 2.6 %collective-permute-start.4 = (f32[24,8]{1,0:T(8,128)S(1)}, f32[24,8]{1,0:T(8,128)S(1)}, u32[]{:S(2)}, u32[]{:S(2)}) collective-permute-start(f32[24,8]{1,0:T(8,128)S(1)} %fusion.18), channel_id=1, source_target_pairs={{0,1},{1,0},{2,3},{3,2},{4,5},{5,4},{6,7},{7,6},{8,9},{9,8},{10,11... | collective-permute-start | bytes 2312 | tf_op jit(solution)/shard_map/ppermute | solution.py:16
  24.0 4.4 %collective-permute-start.5 = (f32[24,8]{1,0:T(8,128)S(1)}, f32[24,8]{1,0:T(8,128)S(1)}, u32[]{:S(2)}, u32[]{:S(2)}) collective-permute-start(f32[24,8]{1,0:T(8,128)S(1)} %add.90), channel_id=1, source_target_pairs={{0,2},{1,3},{2,0},{3,1},{4,6},{5,7},{6,4},{7,5},{8,10},{9,11},{10,... | collective-permute-start | bytes 2312 | tf_op jit(solution)/shard_map/ppermute | solution.py:16
  28.4 5.2 %collective-permute-start.3 = (f32[24,8,128]{2,1,0:T(8,128)S(1)}, f32[24,8,128]{2,1,0:T(8,128)S(1)}, u32[]{:S(2)}, u32[]{:S(2)}) collective-permute-start(f32[24,8,128]{2,1,0:T(8,128)S(1)} %add.88), channel_id=1, source_target_pairs={{0,2},{1,3},{2,0},{3,1},{4,6},{5,7},{6,4},{7,5},{8,10},{9,11},{10,... | collective-permute-start | bytes 294920 | tf_op jit(solution)/shard_map/ppermute | solution.py:16
  102.2 10.2 %all-to-all-start.1 = ((bf16[8,1,3,2048]{3,2,1,0:T(4,128)(2,1)}), bf16[8,1,3,2048]{3,2,1,0:T(4,128)(2,1)S(1)}, u32[]{:S(2)}, u32[]{:S(2)}) async-start(bf16[8,1,3,2048]{3,2,1,0:T(4,128)(2,1)} %copy.43), calls=%async_computation.1 | async-start | bytes 262144 | tf_op jit(solution)/shard_map/all_to_all | solution.py:116
  105.6 134.0 %all-reduce.2.cloned.1.call-start = ((), (), s32[]{:S(2)}) async-start(), calls=%async_computation.2 | async-start | bytes 393216 | tf_op jit(solution)/shard_map/psum | solution.py:124
Sparse Core Ops, SparseCore 0:
  36.0 44.1 all-gather.2
  115.2 124.3 all-reduce.1
